TPU v7x, 256 devices: a whole 4x4x8 slice. The times are simulated.
256 devices in a mesh: view: 32 (over z, y_lo, core), head: 8 (over x, y_hi).
Axes of the slice: x: 4, y: 4 (y_hi: 2, y_lo: 2; y = y_hi * 2 + y_lo), z: 8, core: 2. Of those that a mesh axis runs over, the one named last changes fastest.
Arguments:
- tokens: bfloat16 [8192, 1536], P('view'), may hold values from -8 to 8
- timesteps: int32 [128], P('view'), may hold values from 0 to 999
- adjacency: int32 [128, 6], P('view'), may hold values from 0 to 127, as said below
- neighbour_count: int32 [128], P('view'), may hold values from 2 to 6, as said below
- anchor: int32 [1], replicated, may hold values from 0 to 127
- mod_weight: bfloat16 [256, 6, 1536], P(None, None, 'head'), may hold values from -1.5 to 1.5
- qkv_weight: bfloat16 [1536, 3, 1536], P(None, None, 'head'), may hold values from -1 to 1
- qk_gain: float32 [2, 1536], P(None, 'head'), may hold values from 0.6 to 7.2
- out_weight: bfloat16 [1536, 1536], P('head'), may hold values from -0.15625 to 0.15625
- up_weight: bfloat16 [1536, 6144], P(None, 'head'), may hold values from -0.15625 to 0.15625
- down_weight: bfloat16 [6144, 1536], P('head'), may hold values from -0.078125 to 0.078125
Outputs:
- output: bfloat16 [8192, 1536], P('view')
Inputs may be any that keep to these rules, and one draw needn't show every extreme that they name: `adjacency`: views lie on a closed camera orbit of 128 views (view 128 - 1 beside view 0). Row v names 6 different views other than v, each at most 8 views from v along the orbit; in every draw some used neighbour is exactly 8 views away on each side. Only the first neighbour_count[v] entries are used. `neighbour_count`: some view has 6 neighbours and some view has 2 in every draw.
All inputs are finite; a program needn't handle non-finite values.
Results may differ from a plain program's by a relative error of at most 0.025.
Values may be sent and summed in bfloat16 or wider, within the bound.
A program may use at most 128 MiB of HBM per device.

v0:
```python
import math

import jax
import jax.numpy as jnp
from jax import lax
from jax.sharding import PartitionSpec as P

HD = 64
RADIUS = 8


EPSILON = 1e-06


def shifted(block, axis, distance):
    devices = range(lax.axis_size(axis))
    route = [((i - distance) % len(devices), i) for i in devices]
    return lax.ppermute(block, axis, route)


def from_root(shard, axis, root):
    mine = lax.axis_index(axis) == root
    return lax.psum(jnp.where(mine, shard, jnp.zeros_like(shard)), axis)


def layer_norm(values):
    centre = values - jnp.mean(values, axis=-1, keepdims=True)
    return centre * lax.rsqrt(jnp.mean(centre * centre, axis=-1, keepdims=True) + EPSILON)


def head_norm(values, qk_gains):
    return (
        values * lax.rsqrt(jnp.mean(values * values, axis=-1, keepdims=True) + EPSILON) * qk_gains
    )


def time_features(steps_in, freq_count):
    half_count = freq_count // 2
    frequency = jnp.exp(-math.log(10000.0) * jnp.arange(half_count, dtype=jnp.float32) / half_count)
    angles = steps_in.astype(jnp.float32)[:, None] * frequency[None, :]
    return jnp.concatenate([jnp.cos(angles), jnp.sin(angles)], axis=-1)


def body(
    tokens,
    timesteps,
    adjacency,
    neighbour_count,
    anchor,
    mod_weight,
    qkv_weight,
    qk_gain,
    out_weight,
    up_weight,
    down_weight,
):
    view_count = timesteps.shape[0]
    row_count, model_width = tokens.shape
    view_tokens = row_count // view_count
    local_width = qkv_weight.shape[2]
    local_heads = local_width // HD
    total_views = view_count * lax.axis_size("view")
    first_view = lax.axis_index("view") * view_count
    features = time_features(timesteps, mod_weight.shape[0])
    activated = jax.nn.silu(features).astype(jnp.bfloat16)
    mod_part = jnp.einsum("vf,fsd->vsd", activated, mod_weight, preferred_element_type=jnp.float32)
    modulation = lax.all_gather(mod_part, "head", axis=2, tiled=True)
    inputs = tokens.reshape(view_count, view_tokens, model_width).astype(jnp.float32)
    first_in = (
        layer_norm(inputs) * (1.0 + modulation[:, 1][:, None]) + modulation[:, 0][:, None]
    ).astype(jnp.bfloat16)
    projected = jnp.einsum(
        "vtd,dsc->vtsc", first_in, qkv_weight, preferred_element_type=jnp.float32
    )
    projected = projected.reshape(view_count, view_tokens, 3, local_heads, HD)
    qk_gains = qk_gain.reshape(2, local_heads, HD)
    queries = head_norm(projected[:, :, 0], qk_gains[0]).astype(jnp.bfloat16)
    keys_here = head_norm(projected[:, :, 1], qk_gains[1]).astype(jnp.bfloat16)
    values_here = projected[:, :, 2].astype(jnp.bfloat16)
    kv_block = jnp.concatenate(
        [
            keys_here.reshape(view_count, view_tokens, local_width),
            values_here.reshape(view_count, view_tokens, local_width),
        ],
        axis=-1,
    )
    reach = RADIUS // view_count
    distances = list(range(reach, 0, -1)) + list(range(-1, -reach - 1, -1))
    fetched = [shifted(kv_block, "view", distance) for distance in distances]
    lower_blocks = fetched[:reach]
    upper_blocks = fetched[reach:]
    candidates = jnp.concatenate(lower_blocks + [kv_block] + upper_blocks, axis=0)
    anchor_view = anchor[0]
    owner_index = anchor_view // view_count
    own_piece = lax.dynamic_index_in_dim(kv_block, anchor_view % view_count, 0, keepdims=False)
    anchor_block = from_root(own_piece, "view", owner_index)
    local_ids = jnp.arange(view_count, dtype=jnp.int32)
    global_ids = first_view + local_ids
    half_views = total_views // 2
    offsets = (adjacency - global_ids[:, None] + half_views) % total_views - half_views
    slot_ids = jnp.concatenate(
        [(RADIUS + local_ids)[:, None], RADIUS + local_ids[:, None] + offsets], axis=1
    )
    chosen = candidates[slot_ids]
    anchor_rows = jnp.broadcast_to(anchor_block[None, None], (view_count, 1) + anchor_block.shape)
    gathered = jnp.concatenate([chosen, anchor_rows], axis=1)
    block_count = gathered.shape[1]
    key_blocks = gathered[..., :local_width].reshape(
        view_count, block_count, view_tokens, local_heads, HD
    )
    value_blocks = gathered[..., local_width:].reshape(
        view_count, block_count, view_tokens, local_heads, HD
    )
    usable = jnp.concatenate(
        [
            jnp.ones((view_count, 1), dtype=bool),
            jnp.arange(adjacency.shape[1], dtype=jnp.int32)[None, :] < neighbour_count[:, None],
            jnp.ones((view_count, 1), dtype=bool),
        ],
        axis=1,
    )
    scores = jnp.einsum(
        "vthe,vbshe->vhtbs", queries, key_blocks, preferred_element_type=jnp.float32
    ) * (1.0 / math.sqrt(HD))
    scores = jnp.where(usable[:, None, None, :, None], scores, -jnp.inf)
    largest = jnp.max(scores, axis=(3, 4), keepdims=True)
    powers = jnp.exp(scores - largest)
    weights = (powers / jnp.sum(powers, axis=(3, 4), keepdims=True)).astype(jnp.bfloat16)
    attended = jnp.einsum(
        "vhtbs,vbshe->vthe", weights, value_blocks, preferred_element_type=jnp.float32
    ).astype(jnp.bfloat16)
    attended = attended.reshape(row_count, local_width)
    attn_total = lax.psum(
        jnp.dot(attended, out_weight, preferred_element_type=jnp.float32).astype(jnp.bfloat16),
        "head",
    ).astype(jnp.float32)
    residual = inputs + modulation[:, 2][:, None] * attn_total.reshape(
        view_count, view_tokens, model_width
    )
    second_in = (
        layer_norm(residual) * (1.0 + modulation[:, 4][:, None]) + modulation[:, 3][:, None]
    ).astype(jnp.bfloat16)
    hidden = jax.nn.gelu(
        jnp.dot(
            second_in.reshape(row_count, model_width), up_weight, preferred_element_type=jnp.float32
        ),
        approximate=True,
    ).astype(jnp.bfloat16)
    mlp_total = lax.psum(
        jnp.dot(hidden, down_weight, preferred_element_type=jnp.float32).astype(jnp.bfloat16),
        "head",
    ).astype(jnp.float32)
    finished = residual + modulation[:, 5][:, None] * mlp_total.reshape(
        view_count, view_tokens, model_width
    )
    result = finished.astype(jnp.bfloat16).reshape(row_count, model_width)
    return result


def solution(mesh):
    return jax.shard_map(
        body,
        mesh=mesh,
        in_specs=(
            P("view", None),
            P("view"),
            P("view", None),
            P("view"),
            P(),
            P(None, None, "head"),
            P(None, None, "head"),
            P(None, "head"),
            P("head", None),
            P(None, "head"),
            P("head", None),
        ),
        out_specs=P("view", None),
        check_vma=False,
    )
```

profile of v0, /device:TPU:2, one launch (start us, length us, event | category | flops | bytes accessed | tf_op | source)
XLA Modules:
  0.0 452.5 jit_solution(16673640462495064002)
XLA Ops:
  9.0 65.2 %all_gather.3 = f32[4,6,1536]{1,0,2:T(4,128)S(1)} all-gather(f32[4,6,192]{1,0,2:T(4,128)S(1)} %copy.47), channel_id=1, replica_groups=mesh['view'=32,'head'=8] {'head'}, dimensions={2}, use_global_device_ids=true | all-gather | bytes 165888 | tf_op jit(solution)/shard_map/all_gather | solution.py:67
  74.3 11.9 %fusion.62 = (f32[4,1,1536]{1,0,2:T(4,128)}, f32[4,1,1536]{1,0,2:T(4,128)}, f32[4,1,1536]{1,0,2:T(4,128)}, f32[4,1,1536]{1,0,2:T(4,128)}, f32[4,1,1536]{1,0,2:T(4,128)}, /*index=5*/f32[4,1,1536]{1,0,2:T(4,128)}) fusion(f32[4,6,1536]{1,0,2:T(4,128)S(1)} %all_gather.3), kind=kLoop, calls=%fused_computation.110 | loop fusion | bytes 294912 | tf_op jit(solution)/shard_map/slice | solution.py:153
  86.2 3.1 copy.50
  89.3 3.2 copy.64
  97.8 4.2 collective-permute-start.2
  102.0 2.9 collective-permute-start.3
  114.3 112.5 %psum.21 = bf16[64,384]{0,1:T(8,128)(2,1)} all-reduce(bf16[64,384]{0,1:T(8,128)(2,1)} %fusion.45), channel_id=1, replica_groups=mesh['view'=32,'head'=8] {'view'}, use_global_device_ids=true, to_apply=%region_3.4 | all-reduce | flops 24576 | bytes 98304 | tf_op jit(solution)/shard_map/psum | solution.py:23
  226.8 1.8 constant_dynamic-update-slice_fusion.4
  228.6 1.8 constant_dynamic-update-slice_fusion.3
  231.2 1.8 constant_dynamic-update-slice_fusion.1
  233.0 1.8 constant_dynamic-update-slice_fusion
  234.8 4.0 gather_fusion
  238.9 4.4 fusion.8
  243.2 2.6 copy.53
  245.8 2.1 fusion
  250.8 2.3 convolution_convert_fusion.1
  253.3 3.1 copy.59
  256.4 3.1 copy.65
  259.5 3.1 copy.48
  262.6 82.3 %all-reduce.3.cloned.1.call-done = bf16[256,1536]{1,0:T(8,128)(2,1)} async-done(((bf16[256,1536]{1,0:T(8,128)(2,1)}), bf16[256,1536]{1,0:T(8,128)(2,1)}) %all-reduce.3.cloned.1.call-update) | async-done | bytes 786448 | tf_op jit(solution)/shard_map/psum | solution.py:133
  348.4 4.5 %convolution_convert_fusion = bf16[256,1536]{1,0:T(8,128)(2,1)} fusion(bf16[768,1536]{1,0:T(8,128)(2,1)S(1)} %copy-done, bf16[256,1536]{1,0:T(8,128)(2,1)} %fusion.9, bf16[1536,768]{1,0:T(8,128)(2,1)} %param.20), kind=kOutput, calls=%fused_computation.7 | convolution fusion | flops 1210122240 | bytes 6291456 | tf_op jit(solution)/shard_map/dot_general | solution.py:150
  352.9 3.1 copy.57
  356.1 87.0 %all-reduce.5.cloned.1.call-done = bf16[256,1536]{1,0:T(8,128)(2,1)} async-done(((bf16[256,1536]{1,0:T(8,128)(2,1)}), bf16[256,1536]{1,0:T(8,128)(2,1)}) %all-reduce.5.cloned.1.call-update) | async-done | bytes 786448 | tf_op jit(solution)/shard_map/psum | solution.py:149
  443.0 2.6 fusion.11
  (77 shorter events, 23.7 us)
Async XLA Ops:
  6.5 341.8 %copy-start = (bf16[768,1536]{1,0:T(8,128)(2,1)S(1)}, bf16[768,1536]{1,0:T(8,128)(2,1)}, u32[]{:S(2)}) copy-start(bf16[768,1536]{1,0:T(8,128)(2,1)} %param.21) | copy-start | bytes 7077892
  6.5 338.4 %all-reduce.3.cloned.1.call-start = ((), (), s32[]{:S(2)}) async-start(), calls=%async_computation | async-start | bytes 1572864 | tf_op jit(solution)/shard_map/psum | solution.py:133
  89.3 3.2 copy-start.1
  92.5 1.5 copy-start.9
  94.0 1.2 copy-start.6
  95.1 1.0 copy-start.3
  95.1 12.6 %copy-start.10 = (s32[4]{0:T(128)S(1)}, s32[4]{0:T(128)}, u32[]{:S(2)}) copy-start(s32[4]{0:T(128)} %param.14) | copy-start | bytes 52
  95.1 14.5 %copy-start.7 = (s32[4,6]{1,0:T(4,128)S(1)}, s32[4,6]{1,0:T(4,128)}, u32[]{:S(2)}) copy-start(s32[4,6]{1,0:T(4,128)} %param.13) | copy-start | bytes 292
  97.0 129.8 %collective-permute-start = (bf16[4,64,384]{1,2,0:T(8,128)(2,1)}, bf16[4,64,384]{1,2,0:T(8,128)(2,1)}, u32[]{:S(2)}, u32[]{:S(2)}) collective-permute-start(bf16[4,64,384]{1,2,0:T(8,128)(2,1)} %pad_maximum_fusion.1), channel_id=1, source_target_pairs={{240,0},{248,8},{0,16},{8,24},{16,32},{24,40},{32,48},{40,56},{48,... | collective-permute-start | bytes 589832 | tf_op jit(solution)/shard_map/ppermute | solution.py:18
  97.8 130.7 %collective-permute-start.1 = (bf16[4,64,384]{1,2,0:T(8,128)(2,1)}, bf16[4,64,384]{1,2,0:T(8,128)(2,1)}, u32[]{:S(2)}, u32[]{:S(2)}) collective-permute-start(bf16[4,64,384]{1,2,0:T(8,128)(2,1)} %pad_maximum_fusion.1), channel_id=1, source_target_pairs={{248,0},{0,8},{8,16},{16,24},{24,32},{32,40},{40,48},{48,56},{56,6... | collective-permute-start | bytes 589832 | tf_op jit(solution)/shard_map/ppermute | solution.py:18
  97.8 133.4 %collective-permute-start.2 = (bf16[4,64,384]{1,2,0:T(8,128)(2,1)}, bf16[4,64,384]{1,2,0:T(8,128)(2,1)}, u32[]{:S(2)}, u32[]{:S(2)}) collective-permute-start(bf16[4,64,384]{1,2,0:T(8,128)(2,1)} %pad_maximum_fusion.1), channel_id=1, source_target_pairs={{8,0},{16,8},{24,16},{32,24},{40,32},{48,40},{56,48},{64,56},{72,6... | collective-permute-start | bytes 589832 | tf_op jit(solution)/shard_map/ppermute | solution.py:18
  102.0 131.0 %collective-permute-start.3 = (bf16[4,64,384]{1,2,0:T(8,128)(2,1)}, bf16[4,64,384]{1,2,0:T(8,128)(2,1)}, u32[]{:S(2)}, u32[]{:S(2)}) collective-permute-start(bf16[4,64,384]{1,2,0:T(8,128)(2,1)} %pad_maximum_fusion.1), channel_id=1, source_target_pairs={{16,0},{24,8},{32,16},{40,24},{48,32},{56,40},{64,48},{72,56},{80,... | collective-permute-start | bytes 589832 | tf_op jit(solution)/shard_map/ppermute | solution.py:18
  233.0 5.8 %copy-start.5 = (bf16[64,384]{0,1:T(8,128)(2,1)S(1)}, bf16[64,384]{0,1:T(8,128)(2,1)}, u32[]{:S(2)}) copy-start(bf16[64,384]{0,1:T(8,128)(2,1)} %psum.21) | copy-start | bytes 147460
  243.2 2.6 copy-start.8
  248.0 1.4 copy-start.4
  253.2 189.8 %all-reduce.5.cloned.1.call-start = ((), (), s32[]{:S(2)}) async-start(), calls=%async_computation.1 | async-start | bytes 1572864 | tf_op jit(solution)/shard_map/psum | solution.py:149
  345.0 1.6 copy-start.2
Sparse Core Ops, SparseCore 0:
  253.3 91.5 all-reduce.2
  353.1 89.9 all-reduce.4
where the time goes:
time: 455 us; the launch traced here: 453 us
  blocking collectives  178 us (39%)
  waiting for transfers between devices  169 us (37%)
  local copies, waits for them, and re-layouts  49.1 us (11%)
  other arithmetic  21.6 us (5%)
  between operations  14.3 us (3%)
  matrix products  12.5 us (3%)
  starting transfers between devices  7.93 us (2%)
    psum x1, blocking collectives, from_root(): return lax.psum(jnp.where(mine, shard, jnp.zeros_like(shard)), axis)  112 us
    psum x1, waiting for transfers between devices, body(): lax.psum(jnp.dot(hidden, down_weight, preferred_element_type=jnp.float32)...  87 us
    psum x1, waiting for transfers between devices, body(): lax.psum(jnp.dot(attended, out_weight, preferred_element_type=jnp.float32...  82.3 us
    all_gather x1, blocking collectives, body(): modulation = lax.all_gather(mod_part, 'head', axis=2, tiled=True)  65.2 us
    slice x2, local copies, waits for them, and re-layouts, body(): modulation[:, 5][:, None]  15 us
    unnamed x27, local copies, waits for them, and re-layouts  12.9 us
  transfers between devices with their start and end apart: 6, of which 2 were waited for; matrix products, arithmetic and copies ran while one was open for 6% of the time, Pallas kernels for 0%

commit v1 on v0

v1 whole, which is shorter than its diff:
```python
import functools
import math

import jax
import jax.numpy as jnp
from jax import lax
from jax.experimental import pallas as pl
from jax.experimental.pallas import tpu as pltpu
from jax.sharding import PartitionSpec as P

HD = 64
RADIUS = 8
EPSILON = 1e-06
MESH = pl.DeviceIdType.MESH
F32 = jnp.float32
BF16 = jnp.bfloat16

HEADS_X = 4
HEADS_Y = 2
QUAD = 4

DELTAS = [(2, 1), (1, 1), (3, 1), (2, 0), (0, 1), (1, 0), (3, 0)]


def time_features(steps_in, freq_count):
    half_count = freq_count // 2
    frequency = jnp.exp(-math.log(10000.0) * jnp.arange(half_count, dtype=jnp.float32) / half_count)
    angles = steps_in.astype(jnp.float32)[:, None] * frequency[None, :]
    return jnp.concatenate([jnp.cos(angles), jnp.sin(angles)], axis=-1)


def dot_nt(a, b):
    return lax.dot_general(a, b, (((1,), (1,)), ((), ())), preferred_element_type=F32)


def dot_nn(a, b):
    return lax.dot_general(a, b, (((1,), (0,)), ((), ())), preferred_element_type=F32)


def layer_norm(values):
    centre = values - jnp.mean(values, axis=-1, keepdims=True)
    return centre * lax.rsqrt(jnp.mean(centre * centre, axis=-1, keepdims=True) + EPSILON)


def kernel(
    n_view,
    act_ref,
    gain_ref,
    adj_ref,
    cnt_ref,
    anc_ref,
    tok_hbm,
    modw_hbm,
    qkvw_hbm,
    outw_hbm,
    upw_hbm,
    downw_hbm,
    out_ref,
    tok,
    modw,
    wq,
    wkv,
    outw,
    upw,
    downw,
    normed,
    h1,
    modbuf,
    mods,
    qs,
    kv_own,
    cand,
    kvg,
    anc_src,
    anc_a,
    anc_b,
    anc_bsrc,
    anc_csrc,
    anc_full,
    att,
    part,
    rs1,
    resid,
    h2,
    hidden,
    part2,
    rs2,
    fin,
    ld_sem,
    mod_s,
    mod_r,
    kv_s,
    kv_r,
    aa_s,
    aa_r,
    ab_s,
    ab_r,
    ac_s,
    ac_r,
    rs1_s,
    rs1_r,
    ag1_s,
    ag1_r,
    rs2_s,
    rs2_r,
    ag2_s,
    ag2_r,
):
    v = lax.axis_index("view")
    h = lax.axis_index("head")
    xx, yh = h // HEADS_Y, h % HEADS_Y
    z, q = v // QUAD, v % QUAD
    n_z = n_view // QUAD
    n_head = HEADS_X * HEADS_Y
    width = tok.shape[1]
    rows = tok.shape[0]
    blk = rows // n_head

    def head_peer(dx, dy):
        return ((xx + dx) % HEADS_X) * HEADS_Y + (yh + dy) % HEADS_Y

    def head_dev(dx, dy):
        return (v, head_peer(dx, dy))

    def view_dev(d):
        return ((v + d + n_view) % n_view, h)

    def quad_dev(dq):
        return (z * QUAD + (q + dq) % QUAD, h)

    def z_dev(dz):
        return (((z + dz) % n_z) * QUAD + q, h)

    def rcopy(src, dst, ss, rs, dev):
        return pltpu.make_async_remote_copy(
            src_ref=src, dst_ref=dst, send_sem=ss, recv_sem=rs, device_id=dev, device_id_type=MESH
        )

    barrier = pltpu.get_barrier_semaphore()
    partners = [head_dev(dx, dy) for dx, dy in DELTAS]
    partners += [view_dev(d) for d in (1, -1, 2, -2)]
    partners += [quad_dev(dq) for dq in range(1, QUAD)]
    partners += [z_dev(dz) for dz in range(1, n_z)]
    for dev in partners:
        pl.semaphore_signal(barrier, inc=1, device_id=dev, device_id_type=MESH)

    ld_mod = pltpu.make_async_copy(modw_hbm, modw, ld_sem.at[0])
    ld_mod.start()
    ld_tok = pltpu.make_async_copy(tok_hbm, tok, ld_sem.at[1])
    ld_tok.start()
    zero = jnp.zeros((HD, width), BF16)
    ld_qkv = []
    for i in range(3):
        wq[2 * i * HD + HD : 2 * i * HD + 2 * HD, :] = zero
        outw[2 * i * HD : 2 * i * HD + HD, :] = zero
        for s, (dst, at) in enumerate(
            ((wq, 2 * i * HD), (wkv, 2 * i * HD), (wkv, 2 * i * HD + HD))
        ):
            c = pltpu.make_async_copy(
                qkvw_hbm.at[s, pl.ds(i * HD, HD), :], dst.at[pl.ds(at, HD), :], ld_sem.at[2 + 3 * i + s]
            )
            c.start()
            ld_qkv.append(c)
    ld_out = []
    for i in range(3):
        c = pltpu.make_async_copy(
            outw_hbm.at[pl.ds(i * HD, HD), :], outw.at[pl.ds(2 * i * HD + HD, HD), :], ld_sem.at[11 + i]
        )
        c.start()
        ld_out.append(c)
    ld_up = pltpu.make_async_copy(upw_hbm, upw, ld_sem.at[14])
    ld_up.start()
    ld_down = pltpu.make_async_copy(downw_hbm, downw, ld_sem.at[15])
    ld_down.start()

    ld_mod.wait()
    modbuf[h] = dot_nt(act_ref[...], modw[...])
    pl.semaphore_wait(barrier, len(partners))
    mod_cps = []
    for dx, dy in DELTAS:
        k = dx * HEADS_Y + dy
        c = rcopy(modbuf.at[h], modbuf.at[h], mod_s.at[k], mod_r.at[k], head_dev(dx, dy))
        c.start()
        mod_cps.append(c)

    ld_tok.wait()
    step = 32
    for i in range(rows // step):
        at = slice(i * step, (i + 1) * step)
        normed[at, :] = layer_norm(tok[at, :].astype(F32))

    for c in mod_cps:
        c.wait_recv()
    local_w = modw.shape[0] // 6
    for s in range(6):
        for p in range(n_head):
            mods[s, :, p * local_w : (p + 1) * local_w] = modbuf[p, :, s * local_w : (s + 1) * local_w]

    views = rows // HD
    for j in range(views):
        shift = mods[0, j : j + 1, :]
        scale = 1.0 + mods[1, j : j + 1, :]
        at = slice(j * HD, (j + 1) * HD)
        h1[at, :] = (normed[at, :] * scale + shift).astype(BF16)

    for c in ld_qkv:
        c.wait()
    lane = lax.broadcasted_iota(jnp.int32, (rows, 2 * HD), 1)
    low = lane < HD
    base = (RADIUS // views) * views
    for i in range(3):
        at = slice(2 * i * HD, 2 * (i + 1) * HD)
        kv = dot_nt(h1[...], wkv[at, :])
        gk = gain_ref[1:2, at]
        ms = jnp.sum(jnp.where(low, kv * kv, 0.0), axis=-1, keepdims=True) * (1.0 / HD)
        kv = kv * jnp.where(low, lax.rsqrt(ms + EPSILON) * gk, 1.0)
        kvb = kv.astype(BF16)
        for j in range(views):
            kv_own[j, :, at] = kvb[j * HD : (j + 1) * HD, :]
            cand[base + j, :, at] = kvb[j * HD : (j + 1) * HD, :]

    kv_cps = []
    for i, d in enumerate((2, -2, 1, -1)):
        c = rcopy(kv_own, cand.at[pl.ds(base - d * views, views)], kv_s.at[i], kv_r.at[i], view_dev(d))
        kv_cps.append(c)

    anchor = anc_ref[0]
    piece = kv_own[lax.rem(anchor, views)]
    owners = jnp.zeros(piece.shape, jnp.int32) + lax.div(anchor, views)
    anc_src[...] = jnp.where(owners == v, piece.astype(F32), 0.0).astype(BF16)
    part_rows = HD // QUAD

    def quarter(ref, index):
        return ref.at[pl.ds(pl.multiple_of(index * part_rows, part_rows), part_rows), :]

    a_cps = []
    for dq in (2, 3, 1):
        peer = (q + dq) % QUAD
        c = rcopy(quarter(anc_src, peer), anc_a.at[dq], aa_s.at[dq], aa_r.at[dq], quad_dev(dq))
        c.start()
        a_cps.append(c)
    for c in kv_cps:
        c.start()

    for i in range(3):
        at = slice(2 * i * HD, 2 * (i + 1) * HD)
        qq = dot_nt(h1[...], wq[at, :])
        gq = gain_ref[0:1, at]
        ms = jnp.sum(qq * qq, axis=-1, keepdims=True) * (1.0 / HD)
        qs[:, at] = (qq * (lax.rsqrt(ms + EPSILON) * gq)).astype(BF16)

    for c in a_cps:
        c.wait_recv()
    mine_q = anc_src[pl.ds(pl.multiple_of(q * part_rows, part_rows), part_rows), :]
    anc_bsrc[...] = mine_q + anc_a[1] + anc_a[2] + anc_a[3]
    b_cps = []
    for dz in sorted(range(1, n_z), key=lambda d: -min(d, n_z - d)):
        c = rcopy(anc_bsrc, anc_b.at[dz], ab_s.at[dz], ab_r.at[dz], z_dev(dz))
        c.start()
        b_cps.append(c)
    for c in b_cps:
        c.wait_recv()
    total = anc_bsrc[...]
    for dz in range(1, n_z):
        total = total + anc_b[dz]
    anc_csrc[...] = total
    anc_full[pl.ds(pl.multiple_of(q * part_rows, part_rows), part_rows), :] = total
    c_cps = []
    for dq in (2, 3, 1):
        c = rcopy(anc_csrc, quarter(anc_full, q), ac_s.at[dq], ac_r.at[dq], quad_dev(dq))
        c.start()
        c_cps.append(c)
    for c in kv_cps:
        c.wait_recv()
    for c in c_cps:
        c.wait_recv()

    full_views = n_view * views
    half = full_views // 2
    slots = adj_ref.shape[1]
    keys = (slots + 2) * HD
    cols = cand.shape[2]
    wlane = lax.broadcasted_iota(jnp.int32, (HD, cols), 1)
    klane = lax.broadcasted_iota(jnp.int32, (1, keys), 1)
    for j in range(views):
        kvg[j, 0:HD, :] = kv_own[j]
        gid = v * views + j
        for s in range(slots):
            off = lax.rem(adj_ref[j, s] - gid + half + full_views, full_views) - half
            at = jnp.minimum(jnp.maximum(base + j + off, 0), cand.shape[0] - 1)
            kvg[j, (s + 1) * HD : (s + 2) * HD, :] = cand[at]
        kvg[j, (slots + 1) * HD : (slots + 2) * HD, :] = anc_full[...]
        qv = qs[j * HD : (j + 1) * HD, :]
        none = jnp.zeros_like(qv)
        qb = jnp.concatenate(
            [
                jnp.where((wlane >= 2 * i * HD) & (wlane < 2 * (i + 1) * HD), qv, none)
                for i in range(3)
            ],
            axis=0,
        )
        sc = dot_nt(qb, kvg[j])
        used = (klane < (cnt_ref[j] + 1) * HD) | (klane >= (slots + 1) * HD)
        sc = jnp.where(used, sc, -1e30)
        top = jnp.max(sc, axis=-1, keepdims=True)
        pw = jnp.exp(sc - top)
        den = jnp.sum(pw, axis=-1, keepdims=True)
        ov = dot_nn(pw.astype(BF16), kvg[j]) * (1.0 / den)
        res = jnp.zeros((HD, cols), F32)
        for i in range(3):
            keep = (wlane >= (2 * i + 1) * HD) & (wlane < 2 * (i + 1) * HD)
            res = jnp.where(keep, ov[i * HD : (i + 1) * HD, :], res)
        att[j * HD : (j + 1) * HD, :] = res.astype(BF16)

    for c in ld_out:
        c.wait()
    tile = 256
    for n in range(width // tile):
        at = slice(n * tile, (n + 1) * tile)
        part[:, at] = dot_nn(att[...], outw[:, at]).astype(BF16)

    def block(ref, index):
        return ref.at[pl.ds(pl.multiple_of(index * blk, blk), blk), :]

    r1_cps = []
    for dx, dy in DELTAS:
        k = dx * HEADS_Y + dy
        c = rcopy(block(part, head_peer(dx, dy)), rs1.at[k], rs1_s.at[k], rs1_r.at[k], head_dev(dx, dy))
        c.start()
        r1_cps.append(c)
    my_rows = pl.ds(pl.multiple_of(h * blk, blk), blk)
    per_view = HD // blk
    my_view = h // per_view
    total = part[my_rows, :].astype(F32)
    for c, (dx, dy) in reversed(list(zip(r1_cps, DELTAS))):
        c.wait_recv()
        total = total + rs1[dx * HEADS_Y + dy].astype(F32)

    def mod_row(s):
        return mods[s, pl.ds(my_view, 1), :]

    res = tok[my_rows, :].astype(F32) + mod_row(2) * total
    resid[...] = res
    h2[0] = (layer_norm(res) * (1.0 + mod_row(4)) + mod_row(3)).astype(BF16)
    g1_cps = []
    for dx, dy in DELTAS:
        k = dx * HEADS_Y + dy
        c = rcopy(h2.at[0], h2.at[k], ag1_s.at[k], ag1_r.at[k], head_dev(dx, dy))
        c.start()
        g1_cps.append(c)
    ld_up.wait()
    ld_down.wait()
    for c in g1_cps:
        c.wait_recv()

    ff = upw.shape[1]
    allh2 = jnp.concatenate([h2[k] for k in range(n_head)], axis=0)
    for n in range(ff // tile):
        at = slice(n * tile, (n + 1) * tile)
        u = dot_nn(allh2, upw[:, at])
        hidden[:, at] = (
            0.5 * u * (1.0 + jnp.tanh(math.sqrt(2.0 / math.pi) * (u + 0.044715 * (u * u * u))))
        ).astype(BF16)
    for n in range(width // tile):
        at = slice(n * tile, (n + 1) * tile)
        part2[:, at] = dot_nn(hidden[...], downw[:, at]).astype(BF16)

    r2_cps = []
    for dx, dy in DELTAS:
        k = dx * HEADS_Y + dy
        bx, by = (HEADS_X - dx) % HEADS_X, (HEADS_Y - dy) % HEADS_Y
        c = rcopy(
            part2.at[pl.ds(k * blk, blk), :], rs2.at[k], rs2_s.at[k], rs2_r.at[k], head_dev(bx, by)
        )
        c.start()
        r2_cps.append(c)
    total = part2[0:blk, :].astype(F32)
    for c, (dx, dy) in reversed(list(zip(r2_cps, DELTAS))):
        c.wait_recv()
        total = total + rs2[dx * HEADS_Y + dy].astype(F32)
    done = (resid[...] + mod_row(5) * total).astype(BF16)
    fin[...] = done
    out_ref[my_rows, :] = done
    g2_cps = []
    for dx, dy in DELTAS:
        k = dx * HEADS_Y + dy
        c = rcopy(fin, block(out_ref, h), ag2_s.at[k], ag2_r.at[k], head_dev(dx, dy))
        c.start()
        g2_cps.append(c)
    for c in g2_cps:
        c.wait_recv()
    for c in mod_cps + kv_cps + a_cps + b_cps + c_cps + r1_cps + g1_cps + r2_cps + g2_cps:
        c.wait_send()


def body(
    n_view,
    tokens,
    timesteps,
    adjacency,
    neighbour_count,
    anchor,
    mod_weight,
    qkv_weight,
    qk_gain,
    out_weight,
    up_weight,
    down_weight,
):
    view_count = timesteps.shape[0]
    rows, width = tokens.shape
    freq = mod_weight.shape[0]
    local_w = qkv_weight.shape[2]
    ff = up_weight.shape[1]
    heads = local_w // HD
    cols = 2 * local_w
    act = jax.nn.silu(time_features(timesteps, freq)).astype(BF16)
    act = jnp.pad(act, ((0, 8 - view_count), (0, 0)))
    gains = qk_gain.reshape(2, heads, HD) * jnp.array([1.0 / math.sqrt(HD), 1.0], F32)[:, None, None]
    gains = jnp.pad(gains, ((0, 0), (0, 0), (0, HD))).reshape(2, cols)
    modw = jnp.transpose(mod_weight, (1, 2, 0)).reshape(6 * local_w, freq)
    qkvw = jnp.transpose(qkv_weight, (1, 2, 0))
    n_head = HEADS_X * HEADS_Y
    blk = rows // n_head
    n_z = n_view // QUAD
    reach = RADIUS // view_count
    cand_rows = (2 * reach + 1) * rows
    slots = adjacency.shape[1]
    quarter = HD // QUAD
    vmem = pltpu.VMEM
    dma = pltpu.SemaphoreType.DMA
    scratch = [
        vmem((rows, width), BF16),
        vmem((6 * local_w, freq), BF16),
        vmem((cols, width), BF16),
        vmem((cols, width), BF16),
        vmem((cols, width), BF16),
        vmem((width, ff), BF16),
        vmem((ff, width), BF16),
        vmem((rows, width), F32),
        vmem((rows, width), BF16),
        vmem((n_head, 8, 6 * local_w), F32),
        vmem((6, 8, width), F32),
        vmem((rows, cols), BF16),
        vmem((view_count, HD, cols), BF16),
        vmem((cand_rows // HD, HD, cols), BF16),
        vmem((view_count, (slots + 2) * HD, cols), BF16),
        vmem((HD, cols), BF16),
        vmem((QUAD, quarter, cols), BF16),
        vmem((n_z, quarter, cols), BF16),
        vmem((quarter, cols), BF16),
        vmem((quarter, cols), BF16),
        vmem((HD, cols), BF16),
        vmem((rows, cols), BF16),
        vmem((rows, width), BF16),
        vmem((n_head, blk, width), BF16),
        vmem((blk, width), F32),
        vmem((n_head, blk, width), BF16),
        vmem((rows, ff), BF16),
        vmem((rows, width), BF16),
        vmem((n_head, blk, width), BF16),
        vmem((blk, width), BF16),
        dma((16,)),
        dma((n_head,)),
        dma((n_head,)),
        dma((4,)),
        dma((4,)),
        dma((QUAD,)),
        dma((QUAD,)),
        dma((n_z,)),
        dma((n_z,)),
        dma((QUAD,)),
        dma((QUAD,)),
    ] + [dma((n_head,))] * 8
    return pl.pallas_call(
        functools.partial(kernel, n_view),
        out_shape=jax.ShapeDtypeStruct((rows, width), BF16),
        in_specs=[
            pl.BlockSpec(memory_space=pltpu.VMEM),
            pl.BlockSpec(memory_space=pltpu.VMEM),
            pl.BlockSpec(memory_space=pltpu.SMEM),
            pl.BlockSpec(memory_space=pltpu.SMEM),
            pl.BlockSpec(memory_space=pltpu.SMEM),
        ]
        + [pl.BlockSpec(memory_space=pl.ANY)] * 6,
        out_specs=pl.BlockSpec(memory_space=pltpu.VMEM),
        scratch_shapes=scratch,
        compiler_params=pltpu.CompilerParams(
            collective_id=0, has_side_effects=True, vmem_limit_bytes=52 * 1024 * 1024
        ),
        name="layer",
    )(
        act,
        gains,
        adjacency,
        neighbour_count,
        anchor,
        tokens,
        modw,
        qkvw,
        out_weight,
        up_weight,
        down_weight,
    )


def solution(mesh):
    return jax.shard_map(
        functools.partial(body, mesh.shape["view"]),
        mesh=mesh,
        in_specs=(
            P("view", None),
            P("view"),
            P("view", None),
            P("view"),
            P(),
            P(None, None, "head"),
            P(None, None, "head"),
            P(None, "head"),
            P("head", None),
            P(None, "head"),
            P("head", None),
        ),
        out_specs=P("view", None),
        check_vma=False,
    )
```

time: 455 us -> 92.5 us (0.20)
  the two profiles are of different devices: /device:TPU:2 before, /device:TPU:1 now
where the time goes in v1:
time: 92.5 us; the launch traced here: 92.3 us
  Pallas kernels  84.9 us (92%)
  local copies, waits for them, and re-layouts  5.12 us (6%)
  other arithmetic  1.52 us (2%)
    pallas_call x1, Pallas kernels, body(): pl.pallas_call(functools.partial(kernel, n_view), out_shape=jax.ShapeDtyp...  84.9 us
    unnamed x11, local copies, waits for them, and re-layouts  4.35 us

profile of v1, /device:TPU:1, one launch (start us, length us, event | category | flops | bytes accessed | tf_op | source)
XLA Modules:
  0.0 92.3 jit_solution(11981932349321448288)
XLA Ops:
  0.7 0.7 convert_element_type.10
  1.3 0.1 multiply_cosine_fusion
  1.5 0.8 reshape.16
  2.2 0.7 broadcast_multiply_fusion
  3.0 0.0 copy-start
  3.0 1.1 %copy-done = bf16[256,6,192]{0,2,1:T(8,128)(2,1)S(1)} copy-done((bf16[256,6,192]{0,2,1:T(8,128)(2,1)S(1)}, bf16[256,6,192]{0,2,1:T(8,128)(2,1)}, u32[]{:S(2)}) %copy-start) | copy-done | bytes 589848
  4.0 0.0 copy-start.1
  4.0 1.1 %copy-done.1 = bf16[192,1536]{1,0:T(8,128)(2,1)S(1)} copy-done((bf16[192,1536]{1,0:T(8,128)(2,1)S(1)}, bf16[192,1536]{1,0:T(8,128)(2,1)}, u32[]{:S(2)}) %copy-start.1) | copy-done | bytes 589848
  5.1 0.0 copy-start.2
  5.1 0.7 copy-done.2
  5.8 0.0 copy-start.3
  5.8 0.7 copy-done.3
  6.4 84.9 %layer.1 = bf16[256,1536]{1,0:T(8,128)(2,1)S(1)} custom-call(bf16[8,256]{1,0:T(8,128)(2,1)S(1)} %pad.8.act_ref, f32[2,384]{1,0:T(2,128)S(1)} %bitcast.10, s32[4,6]{1,0:T(4,128)S(1)} %copy-done.2, s32[4]{0:T(128)S(1)} %copy-done.3, s32[1]{0:T(128)S(6)} %copy.17.anc_ref, bf16[256,1536]{1,0:T(8,128)(2,1)} %tok_hbm.1, bf16[1152,256]{1,0:T(8,128)(2,1)S(1)} %bitcast.9, ...), custom_call_target="tpu_custom_call" | custom-call | tf_op jit(solution)/shard_map/layer/pallas_call | solution.py:475
  91.4 0.9 copy.18
  (5 shorter events, 0.0 us)
Async XLA Ops:
  3.0 1.1 %copy-start = (bf16[256,6,192]{0,2,1:T(8,128)(2,1)S(1)}, bf16[256,6,192]{0,2,1:T(8,128)(2,1)}, u32[]{:S(2)}) copy-start(bf16[256,6,192]{0,2,1:T(8,128)(2,1)} %param.17) | copy-start | bytes 1769476
  4.0 1.1 %copy-start.1 = (bf16[192,1536]{1,0:T(8,128)(2,1)S(1)}, bf16[192,1536]{1,0:T(8,128)(2,1)}, u32[]{:S(2)}) copy-start(bf16[192,1536]{1,0:T(8,128)(2,1)} %outw_hbm.1) | copy-start | bytes 1769476
  5.1 0.7 copy-start.2
  5.8 0.7 copy-start.3

commit v2 on v1

--- a/solution.py
+++ b/solution.py
@@ -22,11 +22,22 @@
 DELTAS = [(2, 1), (1, 1), (3, 1), (2, 0), (0, 1), (1, 0), (3, 0)]
 
 
-def time_features(steps_in, freq_count):
-    half_count = freq_count // 2
-    frequency = jnp.exp(-math.log(10000.0) * jnp.arange(half_count, dtype=jnp.float32) / half_count)
-    angles = steps_in.astype(jnp.float32)[:, None] * frequency[None, :]
-    return jnp.concatenate([jnp.cos(angles), jnp.sin(angles)], axis=-1)
+def cos_sin(angle):
+    turns = jnp.floor(angle * (2.0 / math.pi) + 0.5)
+    r = angle - turns * 1.5703125
+    r = r - turns * 4.837512969970703125e-4
+    r = r - turns * 7.54978995489188216e-8
+    s = r * r
+    sin = r + r * s * (-1.6666654611e-1 + s * (8.3321608736e-3 - s * 1.9515295891e-4))
+    cos = 1.0 - 0.5 * s + s * s * (4.166664568298827e-2 + s * (-1.388731625493765e-3 + s * 2.443315711809948e-5))
+    part = turns - 4.0 * jnp.floor(turns * 0.25)
+    odd = (part == 1.0) | (part == 3.0)
+    base_c = jnp.where(odd, sin, cos)
+    base_s = jnp.where(odd, cos, sin)
+    return (
+        jnp.where((part == 1.0) | (part == 2.0), -base_c, base_c),
+        jnp.where((part == 2.0) | (part == 3.0), -base_s, base_s),
+    )
 
 
 def dot_nt(a, b):
@@ -44,11 +55,11 @@
 
 def kernel(
     n_view,
-    act_ref,
-    gain_ref,
-    adj_ref,
-    cnt_ref,
-    anc_ref,
+    ts_hbm,
+    gain_hbm,
+    adj_hbm,
+    cnt_hbm,
+    anc_hbm,
     tok_hbm,
     modw_hbm,
     qkvw_hbm,
@@ -56,6 +67,11 @@
     upw_hbm,
     downw_hbm,
     out_ref,
+    ts_ref,
+    gain_ref,
+    adj_ref,
+    cnt_ref,
+    anc_ref,
     tok,
     modw,
     wq,
@@ -144,10 +160,17 @@
     for dev in partners:
         pl.semaphore_signal(barrier, inc=1, device_id=dev, device_id_type=MESH)
 
+    ld_ts = pltpu.make_async_copy(ts_hbm, ts_ref, ld_sem.at[16])
+    ld_ts.start()
     ld_mod = pltpu.make_async_copy(modw_hbm, modw, ld_sem.at[0])
     ld_mod.start()
     ld_tok = pltpu.make_async_copy(tok_hbm, tok, ld_sem.at[1])
     ld_tok.start()
+    ld_small = []
+    for i, (src, dst) in enumerate(((gain_hbm, gain_ref), (adj_hbm, adj_ref), (cnt_hbm, cnt_ref), (anc_hbm, anc_ref))):
+        c = pltpu.make_async_copy(src, dst, ld_sem.at[17 + i])
+        c.start()
+        ld_small.append(c)
     zero = jnp.zeros((HD, width), BF16)
     ld_qkv = []
     for i in range(3):
@@ -173,8 +196,23 @@
     ld_down = pltpu.make_async_copy(downw_hbm, downw, ld_sem.at[15])
     ld_down.start()
 
+    views = rows // HD
+    ld_ts.wait()
+    half_freq = modw.shape[1] // 2
+    row8 = lax.broadcasted_iota(jnp.int32, (8, half_freq), 0)
+    times = jnp.zeros((8, half_freq), jnp.int32)
+    for j in range(views):
+        times = jnp.where((row8 == j) | (row8 == j + 4), ts_ref[j], times)
+    steps = lax.broadcasted_iota(jnp.int32, (8, half_freq), 1).astype(F32)
+    cos, sin = cos_sin(times.astype(F32) * jnp.exp(steps * (-math.log(10000.0) / half_freq)))
+    feats = jnp.concatenate([cos, sin], axis=1)
+    act = (feats / (1.0 + jnp.exp(-feats))).astype(BF16)
     ld_mod.wait()
-    modbuf[h] = dot_nt(act_ref[...], modw[...])
+    local_w = modw.shape[0] // 6
+    first = dot_nt(act, modw[0 : 3 * local_w, :])
+    second = dot_nt(act, modw[3 * local_w : 6 * local_w, :])
+    row8w = lax.broadcasted_iota(jnp.int32, first.shape, 0)
+    modbuf[h] = jnp.where(row8w < 4, first, second).astype(BF16)
     pl.semaphore_wait(barrier, len(partners))
     mod_cps = []
     for dx, dy in DELTAS:
@@ -191,19 +229,18 @@
 
     for c in mod_cps:
         c.wait_recv()
-    local_w = modw.shape[0] // 6
-    for s in range(6):
-        for p in range(n_head):
-            mods[s, :, p * local_w : (p + 1) * local_w] = modbuf[p, :, s * local_w : (s + 1) * local_w]
-
-    views = rows // HD
+    for p in range(n_head):
+        got = modbuf[p].astype(F32)
+        for s in range(3):
+            mods[s, :, p * local_w : (p + 1) * local_w] = got[:, s * local_w : (s + 1) * local_w]
+
     for j in range(views):
         shift = mods[0, j : j + 1, :]
         scale = 1.0 + mods[1, j : j + 1, :]
         at = slice(j * HD, (j + 1) * HD)
         h1[at, :] = (normed[at, :] * scale + shift).astype(BF16)
 
-    for c in ld_qkv:
+    for c in ld_qkv + ld_small:
         c.wait()
     lane = lax.broadcasted_iota(jnp.int32, (rows, 2 * HD), 1)
     low = lane < HD
@@ -211,7 +248,7 @@
     for i in range(3):
         at = slice(2 * i * HD, 2 * (i + 1) * HD)
         kv = dot_nt(h1[...], wkv[at, :])
-        gk = gain_ref[1:2, at]
+        gk = jnp.concatenate([gain_ref[1:2, i * HD : (i + 1) * HD], jnp.ones((1, HD), F32)], axis=1)
         ms = jnp.sum(jnp.where(low, kv * kv, 0.0), axis=-1, keepdims=True) * (1.0 / HD)
         kv = kv * jnp.where(low, lax.rsqrt(ms + EPSILON) * gk, 1.0)
         kvb = kv.astype(BF16)
@@ -219,10 +256,31 @@
             kv_own[j, :, at] = kvb[j * HD : (j + 1) * HD, :]
             cand[base + j, :, at] = kvb[j * HD : (j + 1) * HD, :]
 
+    core = v % 2
+    mate = view_dev(1 - 2 * core)
     kv_cps = []
-    for i, d in enumerate((2, -2, 1, -1)):
-        c = rcopy(kv_own, cand.at[pl.ds(base - d * views, views)], kv_s.at[i], kv_r.at[i], view_dev(d))
-        kv_cps.append(c)
+    fwd_cps = []
+
+    def send_kv(j):
+        for i, (dst, dev) in enumerate(
+            (
+                (base - 2 * views + j, view_dev(2)),
+                (base + 2 * views + j, view_dev(-2)),
+                (base - views + 2 * views * core + j, mate),
+            )
+        ):
+            c = rcopy(kv_own.at[j], cand.at[dst], kv_s.at[i, j], kv_r.at[i, j], dev)
+            c.start()
+            kv_cps.append(c)
+
+    def forward_kv(j):
+        got = base + 2 * views - 4 * views * core + j
+        rcopy(kv_own.at[j], cand.at[got], kv_s.at[0, j], kv_r.at[1 - core, j], mate).wait_recv()
+        c = rcopy(
+            cand.at[got], cand.at[base + views - 2 * views * core + j], kv_s.at[3, j], kv_r.at[3, j], mate
+        )
+        c.start()
+        fwd_cps.append(c)
 
     anchor = anc_ref[0]
     piece = kv_own[lax.rem(anchor, views)]
@@ -239,13 +297,14 @@
         c = rcopy(quarter(anc_src, peer), anc_a.at[dq], aa_s.at[dq], aa_r.at[dq], quad_dev(dq))
         c.start()
         a_cps.append(c)
-    for c in kv_cps:
-        c.start()
+    send_kv(0)
+    send_kv(1)
 
     for i in range(3):
         at = slice(2 * i * HD, 2 * (i + 1) * HD)
         qq = dot_nt(h1[...], wq[at, :])
-        gq = gain_ref[0:1, at]
+        gq = gain_ref[0:1, i * HD : (i + 1) * HD] * (1.0 / math.sqrt(HD))
+        gq = jnp.concatenate([gq, jnp.zeros((1, HD), F32)], axis=1)
         ms = jnp.sum(qq * qq, axis=-1, keepdims=True) * (1.0 / HD)
         qs[:, at] = (qq * (lax.rsqrt(ms + EPSILON) * gq)).astype(BF16)
 
@@ -258,6 +317,10 @@
         c = rcopy(anc_bsrc, anc_b.at[dz], ab_s.at[dz], ab_r.at[dz], z_dev(dz))
         c.start()
         b_cps.append(c)
+    for j in range(2, views):
+        send_kv(j)
+    forward_kv(0)
+    forward_kv(1)
     for c in b_cps:
         c.wait_recv()
     total = anc_bsrc[...]
@@ -270,8 +333,13 @@
         c = rcopy(anc_csrc, quarter(anc_full, q), ac_s.at[dq], ac_r.at[dq], quad_dev(dq))
         c.start()
         c_cps.append(c)
-    for c in kv_cps:
-        c.wait_recv()
+    for j in range(2, views):
+        forward_kv(j)
+    for j in range(views):
+        got = base - 2 * views + 4 * views * core + j
+        rcopy(kv_own.at[j], cand.at[got], kv_s.at[0, j], kv_r.at[core, j], mate).wait_recv()
+        kv_cps[3 * j + 2].wait_recv()
+        fwd_cps[j].wait_recv()
     for c in c_cps:
         c.wait_recv()
 
@@ -337,7 +405,7 @@
         total = total + rs1[dx * HEADS_Y + dy].astype(F32)
 
     def mod_row(s):
-        return mods[s, pl.ds(my_view, 1), :]
+        return mods[s % 3, pl.ds(my_view + 4 * (s // 3), 1), :]
 
     res = tok[my_rows, :].astype(F32) + mod_row(2) * total
     resid[...] = res
@@ -389,7 +457,7 @@
         g2_cps.append(c)
     for c in g2_cps:
         c.wait_recv()
-    for c in mod_cps + kv_cps + a_cps + b_cps + c_cps + r1_cps + g1_cps + r2_cps + g2_cps:
+    for c in mod_cps + kv_cps + fwd_cps + a_cps + b_cps + c_cps + r1_cps + g1_cps + r2_cps + g2_cps:
         c.wait_send()
 
 
@@ -412,12 +480,7 @@
     freq = mod_weight.shape[0]
     local_w = qkv_weight.shape[2]
     ff = up_weight.shape[1]
-    heads = local_w // HD
     cols = 2 * local_w
-    act = jax.nn.silu(time_features(timesteps, freq)).astype(BF16)
-    act = jnp.pad(act, ((0, 8 - view_count), (0, 0)))
-    gains = qk_gain.reshape(2, heads, HD) * jnp.array([1.0 / math.sqrt(HD), 1.0], F32)[:, None, None]
-    gains = jnp.pad(gains, ((0, 0), (0, 0), (0, HD))).reshape(2, cols)
     modw = jnp.transpose(mod_weight, (1, 2, 0)).reshape(6 * local_w, freq)
     qkvw = jnp.transpose(qkv_weight, (1, 2, 0))
     n_head = HEADS_X * HEADS_Y
@@ -430,6 +493,11 @@
     vmem = pltpu.VMEM
     dma = pltpu.SemaphoreType.DMA
     scratch = [
+        pltpu.SMEM(timesteps.shape, jnp.int32),
+        vmem(qk_gain.shape, F32),
+        pltpu.SMEM(adjacency.shape, jnp.int32),
+        pltpu.SMEM(neighbour_count.shape, jnp.int32),
+        pltpu.SMEM(anchor.shape, jnp.int32),
         vmem((rows, width), BF16),
         vmem((6 * local_w, freq), BF16),
         vmem((cols, width), BF16),
@@ -439,8 +507,8 @@
         vmem((ff, width), BF16),
         vmem((rows, width), F32),
         vmem((rows, width), BF16),
-        vmem((n_head, 8, 6 * local_w), F32),
-        vmem((6, 8, width), F32),
+        vmem((n_head, 8, 3 * local_w), BF16),
+        vmem((3, 8, width), F32),
         vmem((rows, cols), BF16),
         vmem((view_count, HD, cols), BF16),
         vmem((cand_rows // HD, HD, cols), BF16),
@@ -460,11 +528,11 @@
         vmem((rows, width), BF16),
         vmem((n_head, blk, width), BF16),
         vmem((blk, width), BF16),
-        dma((16,)),
+        dma((21,)),
         dma((n_head,)),
         dma((n_head,)),
-        dma((4,)),
-        dma((4,)),
+        dma((4, view_count)),
+        dma((4, view_count)),
         dma((QUAD,)),
         dma((QUAD,)),
         dma((n_z,)),
@@ -475,23 +543,16 @@
     return pl.pallas_call(
         functools.partial(kernel, n_view),
         out_shape=jax.ShapeDtypeStruct((rows, width), BF16),
-        in_specs=[
-            pl.BlockSpec(memory_space=pltpu.VMEM),
-            pl.BlockSpec(memory_space=pltpu.VMEM),
-            pl.BlockSpec(memory_space=pltpu.SMEM),
-            pl.BlockSpec(memory_space=pltpu.SMEM),
-            pl.BlockSpec(memory_space=pltpu.SMEM),
-        ]
-        + [pl.BlockSpec(memory_space=pl.ANY)] * 6,
+        in_specs=[pl.BlockSpec(memory_space=pl.ANY)] * 11,
         out_specs=pl.BlockSpec(memory_space=pltpu.VMEM),
         scratch_shapes=scratch,
         compiler_params=pltpu.CompilerParams(
-            collective_id=0, has_side_effects=True, vmem_limit_bytes=52 * 1024 * 1024
+            collective_id=0, has_side_effects=True, vmem_limit_bytes=67043328
         ),
         name="layer",
     )(
-        act,
-        gains,
+        timesteps,
+        qk_gain,
         adjacency,
         neighbour_count,
         anchor,

time: 92.5 us -> 83.4 us (0.902)
  Pallas kernels: 84.9 us -> 80.5 us
  local copies, waits for them, and re-layouts: 5.12 us -> 2.06 us
  other arithmetic: 1.52 us -> 0 us
    pallas_call x1, Pallas kernels: 84.9 us -> 80.5 us  [body(): pl.pallas_call(functools.partial(kernel, n_view), out_shape=jax.ShapeDtyp...]
    unnamed x11 -> x1, local copies, waits for them, and re-layouts: 4.35 us -> 2.06 us
where the time goes in v2:
time: 83.4 us; the launch traced here: 83.2 us
  Pallas kernels  80.5 us (97%)
  local copies, waits for them, and re-layouts  2.06 us (2%)
    pallas_call x1, Pallas kernels, body(): pl.pallas_call(functools.partial(kernel, n_view), out_shape=jax.ShapeDtyp...  80.5 us
    unnamed x1, local copies, waits for them, and re-layouts  2.06 us

profile of v2, /device:TPU:1, one launch (start us, length us, event | category | flops | bytes accessed | tf_op | source)
XLA Modules:
  0.0 83.2 jit_solution(12612542252434511065)
XLA Ops:
  0.7 80.5 %layer.1 = bf16[256,1536]{1,0:T(8,128)(2,1)} custom-call(s32[4]{0:T(128)} %ts_hbm.1, f32[2,192]{1,0:T(2,128)} %gain_hbm.1, s32[4,6]{1,0:T(4,128)} %adj_hbm.1, s32[4]{0:T(128)} %cnt_hbm.1, s32[1]{0:T(128)S(6)} %copy.13.anc_hbm, bf16[256,1536]{1,0:T(8,128)(2,1)} %tok_hbm.1, bf16[1152,256]{1,0:T(8,128)(2,1)} %bitcast.5, bf16[3,192,1536]{2,1,0:T(8,128)(2,1)} %bitcast.4, ...), custom_call_target="tpu_custom_call" | custom-call | tf_op jit(solution)/shard_map/layer/pallas_call | solution.py:543
  81.2 2.1 %copy.14 = bf16[256,1536]{1,0:T(8,128)(2,1)} copy(bf16[256,1536]{1,0:T(8,128)(2,1)} %layer.1) | data formatting | bytes 1572864

commit v3 on v2

--- a/solution.py
+++ b/solution.py
@@ -18,6 +18,7 @@
 HEADS_X = 4
 HEADS_Y = 2
 QUAD = 4
+CHUNKS = 2
 
 DELTAS = [(2, 1), (1, 1), (3, 1), (2, 0), (0, 1), (1, 0), (3, 0)]
 
@@ -130,7 +131,6 @@
     n_head = HEADS_X * HEADS_Y
     width = tok.shape[1]
     rows = tok.shape[0]
-    blk = rows // n_head
 
     def head_peer(dx, dy):
         return ((xx + dx) % HEADS_X) * HEADS_Y + (yh + dy) % HEADS_Y
@@ -350,7 +350,7 @@
     cols = cand.shape[2]
     wlane = lax.broadcasted_iota(jnp.int32, (HD, cols), 1)
     klane = lax.broadcasted_iota(jnp.int32, (1, keys), 1)
-    for j in range(views):
+    def attention(j):
         kvg[j, 0:HD, :] = kv_own[j]
         gid = v * views + j
         for s in range(slots):
@@ -380,84 +380,102 @@
             res = jnp.where(keep, ov[i * HD : (i + 1) * HD, :], res)
         att[j * HD : (j + 1) * HD, :] = res.astype(BF16)
 
+    tile = 256
+    crows = rows // CHUNKS
+    blk = crows // n_head
+    ff = upw.shape[1]
+
+    def rows_at(start, size):
+        return pl.ds(pl.multiple_of(start, size), size)
+
+    def mod_row(s, view):
+        return mods[s % 3, pl.ds(view + 4 * (s // 3), 1), :]
+
+    r1_cps, g1_cps, r2_cps, g2_cps = ([[] for _ in range(CHUNKS)] for _ in range(4))
+
+    def project(c):
+        span = slice(c * crows, (c + 1) * crows)
+        for n in range(width // tile):
+            at = slice(n * tile, (n + 1) * tile)
+            part[span, at] = dot_nn(att[span, :], outw[:, at]).astype(BF16)
+        for dx, dy in DELTAS:
+            k = dx * HEADS_Y + dy
+            src = part.at[rows_at(c * crows + head_peer(dx, dy) * blk, blk), :]
+            r1_cps[c].append(rcopy(src, rs1.at[k, c], rs1_s.at[k, c], rs1_r.at[k, c], head_dev(dx, dy)))
+            r1_cps[c][-1].start()
+
+    def second_norm(c):
+        mine = rows_at(c * crows + h * blk, blk)
+        view = (c * crows + h * blk) // HD
+        total = part[mine, :].astype(F32)
+        for cp in reversed(r1_cps[c]):
+            cp.wait_recv()
+        for k in range(1, n_head):
+            total = total + rs1[k, c].astype(F32)
+        res = tok[mine, :].astype(F32) + mod_row(2, view) * total
+        resid[c] = res
+        h2[c, 0:blk, :] = (layer_norm(res) * (1.0 + mod_row(4, view)) + mod_row(3, view)).astype(BF16)
+        for dx, dy in DELTAS:
+            k = dx * HEADS_Y + dy
+            src, dst = h2.at[c, pl.ds(0, blk), :], h2.at[c, pl.ds(k * blk, blk), :]
+            g1_cps[c].append(rcopy(src, dst, ag1_s.at[k, c], ag1_r.at[k, c], head_dev(dx, dy)))
+            g1_cps[c][-1].start()
+
+    def feed_forward(c):
+        for cp in reversed(g1_cps[c]):
+            cp.wait_recv()
+        span = slice(c * crows, (c + 1) * crows)
+        for n in range(ff // tile):
+            at = slice(n * tile, (n + 1) * tile)
+            u = dot_nn(h2[c], upw[:, at])
+            hidden[span, at] = (
+                0.5 * u * (1.0 + jnp.tanh(math.sqrt(2.0 / math.pi) * (u + 0.044715 * (u * u * u))))
+            ).astype(BF16)
+        for n in range(width // tile):
+            at = slice(n * tile, (n + 1) * tile)
+            part2[span, at] = dot_nn(hidden[span, :], downw[:, at]).astype(BF16)
+        for dx, dy in DELTAS:
+            bx, by = (HEADS_X - dx) % HEADS_X, (HEADS_Y - dy) % HEADS_Y
+            k = bx * HEADS_Y + by
+            src = part2.at[pl.ds(c * crows + k * blk, blk), :]
+            r2_cps[c].append(rcopy(src, rs2.at[k, c], rs2_s.at[k, c], rs2_r.at[k, c], head_dev(dx, dy)))
+            r2_cps[c][-1].start()
+
+    def finish(c):
+        view = (c * crows + h * blk) // HD
+        total = part2[c * crows : c * crows + blk, :].astype(F32)
+        for cp in reversed(r2_cps[c]):
+            cp.wait_recv()
+        for k in range(1, n_head):
+            total = total + rs2[k, c].astype(F32)
+        done = (resid[c] + mod_row(5, view) * total).astype(BF16)
+        fin[c] = done
+        mine = rows_at(c * crows + h * blk, blk)
+        out_ref[mine, :] = done
+        for dx, dy in DELTAS:
+            k = dx * HEADS_Y + dy
+            g2_cps[c].append(rcopy(fin.at[c], out_ref.at[mine, :], ag2_s.at[k, c], ag2_r.at[k, c], head_dev(dx, dy)))
+            g2_cps[c][-1].start()
+
     for c in ld_out:
         c.wait()
-    tile = 256
-    for n in range(width // tile):
-        at = slice(n * tile, (n + 1) * tile)
-        part[:, at] = dot_nn(att[...], outw[:, at]).astype(BF16)
-
-    def block(ref, index):
-        return ref.at[pl.ds(pl.multiple_of(index * blk, blk), blk), :]
-
-    r1_cps = []
-    for dx, dy in DELTAS:
-        k = dx * HEADS_Y + dy
-        c = rcopy(block(part, head_peer(dx, dy)), rs1.at[k], rs1_s.at[k], rs1_r.at[k], head_dev(dx, dy))
-        c.start()
-        r1_cps.append(c)
-    my_rows = pl.ds(pl.multiple_of(h * blk, blk), blk)
-    per_view = HD // blk
-    my_view = h // per_view
-    total = part[my_rows, :].astype(F32)
-    for c, (dx, dy) in reversed(list(zip(r1_cps, DELTAS))):
-        c.wait_recv()
-        total = total + rs1[dx * HEADS_Y + dy].astype(F32)
-
-    def mod_row(s):
-        return mods[s % 3, pl.ds(my_view + 4 * (s // 3), 1), :]
-
-    res = tok[my_rows, :].astype(F32) + mod_row(2) * total
-    resid[...] = res
-    h2[0] = (layer_norm(res) * (1.0 + mod_row(4)) + mod_row(3)).astype(BF16)
-    g1_cps = []
-    for dx, dy in DELTAS:
-        k = dx * HEADS_Y + dy
-        c = rcopy(h2.at[0], h2.at[k], ag1_s.at[k], ag1_r.at[k], head_dev(dx, dy))
-        c.start()
-        g1_cps.append(c)
+    for c in range(CHUNKS):
+        for j in range(c * crows // HD, (c + 1) * crows // HD):
+            attention(j)
+        project(c)
+    for c in range(CHUNKS):
+        second_norm(c)
     ld_up.wait()
     ld_down.wait()
-    for c in g1_cps:
-        c.wait_recv()
-
-    ff = upw.shape[1]
-    allh2 = jnp.concatenate([h2[k] for k in range(n_head)], axis=0)
-    for n in range(ff // tile):
-        at = slice(n * tile, (n + 1) * tile)
-        u = dot_nn(allh2, upw[:, at])
-        hidden[:, at] = (
-            0.5 * u * (1.0 + jnp.tanh(math.sqrt(2.0 / math.pi) * (u + 0.044715 * (u * u * u))))
-        ).astype(BF16)
-    for n in range(width // tile):
-        at = slice(n * tile, (n + 1) * tile)
-        part2[:, at] = dot_nn(hidden[...], downw[:, at]).astype(BF16)
-
-    r2_cps = []
-    for dx, dy in DELTAS:
-        k = dx * HEADS_Y + dy
-        bx, by = (HEADS_X - dx) % HEADS_X, (HEADS_Y - dy) % HEADS_Y
-        c = rcopy(
-            part2.at[pl.ds(k * blk, blk), :], rs2.at[k], rs2_s.at[k], rs2_r.at[k], head_dev(bx, by)
-        )
-        c.start()
-        r2_cps.append(c)
-    total = part2[0:blk, :].astype(F32)
-    for c, (dx, dy) in reversed(list(zip(r2_cps, DELTAS))):
-        c.wait_recv()
-        total = total + rs2[dx * HEADS_Y + dy].astype(F32)
-    done = (resid[...] + mod_row(5) * total).astype(BF16)
-    fin[...] = done
-    out_ref[my_rows, :] = done
-    g2_cps = []
-    for dx, dy in DELTAS:
-        k = dx * HEADS_Y + dy
-        c = rcopy(fin, block(out_ref, h), ag2_s.at[k], ag2_r.at[k], head_dev(dx, dy))
-        c.start()
-        g2_cps.append(c)
-    for c in g2_cps:
-        c.wait_recv()
-    for c in mod_cps + kv_cps + fwd_cps + a_cps + b_cps + c_cps + r1_cps + g1_cps + r2_cps + g2_cps:
+    for c in range(CHUNKS):
+        feed_forward(c)
+    for c in range(CHUNKS):
+        finish(c)
+    for c in range(CHUNKS):
+        for cp in g2_cps[c]:
+            cp.wait_recv()
+    rest = [cp for phase in (r1_cps, g1_cps, r2_cps, g2_cps) for group in phase for cp in group]
+    for c in mod_cps + kv_cps + fwd_cps + a_cps + b_cps + c_cps + rest:
         c.wait_send()
 
 
@@ -484,7 +502,7 @@
     modw = jnp.transpose(mod_weight, (1, 2, 0)).reshape(6 * local_w, freq)
     qkvw = jnp.transpose(qkv_weight, (1, 2, 0))
     n_head = HEADS_X * HEADS_Y
-    blk = rows // n_head
+    blk = rows // n_head // CHUNKS
     n_z = n_view // QUAD
     reach = RADIUS // view_count
     cand_rows = (2 * reach + 1) * rows
@@ -521,13 +539,13 @@
         vmem((HD, cols), BF16),
         vmem((rows, cols), BF16),
         vmem((rows, width), BF16),
-        vmem((n_head, blk, width), BF16),
-        vmem((blk, width), F32),
-        vmem((n_head, blk, width), BF16),
+        vmem((n_head, CHUNKS, blk, width), BF16),
+        vmem((CHUNKS, blk, width), F32),
+        vmem((CHUNKS, n_head * blk, width), BF16),
         vmem((rows, ff), BF16),
         vmem((rows, width), BF16),
-        vmem((n_head, blk, width), BF16),
-        vmem((blk, width), BF16),
+        vmem((n_head, CHUNKS, blk, width), BF16),
+        vmem((CHUNKS, blk, width), BF16),
         dma((21,)),
         dma((n_head,)),
         dma((n_head,)),
@@ -539,7 +557,7 @@
         dma((n_z,)),
         dma((QUAD,)),
         dma((QUAD,)),
-    ] + [dma((n_head,))] * 8
+    ] + [dma((n_head, CHUNKS))] * 8
     return pl.pallas_call(
         functools.partial(kernel, n_view),
         out_shape=jax.ShapeDtypeStruct((rows, width), BF16),

time: 83.4 us -> 71.6 us (0.86)
  the two profiles are of different devices: /device:TPU:1 before, /device:TPU:2 now
where the time goes in v3:
time: 71.6 us; the launch traced here: 70.6 us
  Pallas kernels  67.9 us (95%)
  local copies, waits for them, and re-layouts  2.06 us (3%)
    pallas_call x1, Pallas kernels, body(): pl.pallas_call(functools.partial(kernel, n_view), out_shape=jax.ShapeDtyp...  67.9 us
    unnamed x1, local copies, waits for them, and re-layouts  2.06 us

profile of v3, /device:TPU:2, one launch (start us, length us, event | category | flops | bytes accessed | tf_op | source)
XLA Modules:
  0.0 70.6 jit_solution(6095321436688685480)
XLA Ops:
  0.7 67.9 %layer.1 = bf16[256,1536]{1,0:T(8,128)(2,1)} custom-call(s32[4]{0:T(128)} %ts_hbm.1, f32[2,192]{1,0:T(2,128)} %gain_hbm.1, s32[4,6]{1,0:T(4,128)} %adj_hbm.1, s32[4]{0:T(128)} %cnt_hbm.1, s32[1]{0:T(128)S(6)} %copy.13.anc_hbm, bf16[256,1536]{1,0:T(8,128)(2,1)} %tok_hbm.1, bf16[1152,256]{1,0:T(8,128)(2,1)} %bitcast.5, bf16[3,192,1536]{2,1,0:T(8,128)(2,1)} %bitcast.4, ...), custom_call_target="tpu_custom_call" | custom-call | tf_op jit(solution)/shard_map/layer/pallas_call | solution.py:561
  68.5 2.1 %copy.14 = bf16[256,1536]{1,0:T(8,128)(2,1)} copy(bf16[256,1536]{1,0:T(8,128)(2,1)} %layer.1) | data formatting | bytes 1572864

commit v4 on v3

--- a/solution.py
+++ b/solution.py
@@ -21,6 +21,13 @@
 CHUNKS = 2
 
 DELTAS = [(2, 1), (1, 1), (3, 1), (2, 0), (0, 1), (1, 0), (3, 0)]
+SPREAD = [(0, 1), (2, 0), (1, 0), (3, 0)]
+FORWARDS = [((0, 1), [(1, 0), (3, 0)]), ((2, 0), [(0, 1)])]
+RELAYED = [(4, (2, 1), (0, 1)), (2, (1, 1), (1, 0)), (3, (3, 1), (3, 0))]
+DIRECT = [(0, (1, 0), (1, 0)), (1, (3, 0), (3, 0))]
+MIXED = [(6, (2, 0), (4,)), (5, (0, 1), (2, 3))]
+FINAL = [0, 1, 6, 5]
+LAG = 0.2
 
 
 def cos_sin(angle):
@@ -96,12 +103,12 @@
     anc_full,
     att,
     part,
-    rs1,
+    rs,
+    mix,
     resid,
     h2,
     hidden,
     part2,
-    rs2,
     fin,
     ld_sem,
     mod_s,
@@ -114,12 +121,10 @@
     ab_r,
     ac_s,
     ac_r,
-    rs1_s,
-    rs1_r,
     ag1_s,
     ag1_r,
-    rs2_s,
-    rs2_r,
+    rs_s,
+    rs_r,
     ag2_s,
     ag2_r,
 ):
@@ -391,39 +396,89 @@
     def mod_row(s, view):
         return mods[s % 3, pl.ds(view + 4 * (s // 3), 1), :]
 
-    r1_cps, g1_cps, r2_cps, g2_cps = ([[] for _ in range(CHUNKS)] for _ in range(4))
+    g1_cps, g2_cps = ([[] for _ in range(CHUNKS)] for _ in range(2))
+    rs_cps = [[{} for _ in range(CHUNKS)] for _ in range(2)]
+
+    def block_for(phase, c, dx, dy):
+        if phase == 0:
+            return part.at[rows_at(c * crows + head_peer(dx, dy) * blk, blk), :]
+        k = (HEADS_X - dx) % HEADS_X * HEADS_Y + (HEADS_Y - dy) % HEADS_Y
+        return part2.at[pl.ds(c * crows + k * blk, blk), :]
+
+    def scatter(phase, c, slot, src, dx, dy):
+        cp = rcopy(src, rs.at[phase, c, slot], rs_s.at[phase, c, slot], rs_r.at[phase, c, slot], head_dev(dx, dy))
+        cp.start()
+        rs_cps[phase][c][slot] = cp
+
+    def scatter_first(phase, c):
+        for slot, owner, hop in RELAYED + DIRECT:
+            scatter(phase, c, slot, block_for(phase, c, *owner), *hop)
+
+    def scatter_second(phase, c):
+        for i, (slot, hop, parts) in enumerate(MIXED):
+            total = block_for(phase, c, *hop)[...].astype(F32)
+            for p in parts:
+                rs_cps[phase][c][p].wait_recv()
+                total = total + rs[phase, c, p].astype(F32)
+            mix[phase, c, i] = total.astype(BF16)
+            scatter(phase, c, slot, mix.at[phase, c, i], *hop)
+
+    def scatter_sum(phase, c):
+        total = block_for(phase, c, 0, 0)[...].astype(F32)
+        for slot in FINAL:
+            rs_cps[phase][c][slot].wait_recv()
+            total = total + rs[phase, c, slot].astype(F32)
+        return total
 
     def project(c):
+        for j in range(c * crows // HD, (c + 1) * crows // HD):
+            attention(j)
         span = slice(c * crows, (c + 1) * crows)
         for n in range(width // tile):
             at = slice(n * tile, (n + 1) * tile)
             part[span, at] = dot_nn(att[span, :], outw[:, at]).astype(BF16)
-        for dx, dy in DELTAS:
-            k = dx * HEADS_Y + dy
-            src = part.at[rows_at(c * crows + head_peer(dx, dy) * blk, blk), :]
-            r1_cps[c].append(rcopy(src, rs1.at[k, c], rs1_s.at[k, c], rs1_r.at[k, c], head_dev(dx, dy)))
-            r1_cps[c][-1].start()
+        scatter_first(0, c)
 
     def second_norm(c):
         mine = rows_at(c * crows + h * blk, blk)
         view = (c * crows + h * blk) // HD
-        total = part[mine, :].astype(F32)
-        for cp in reversed(r1_cps[c]):
-            cp.wait_recv()
-        for k in range(1, n_head):
-            total = total + rs1[k, c].astype(F32)
+        total = scatter_sum(0, c)
         res = tok[mine, :].astype(F32) + mod_row(2, view) * total
         resid[c] = res
         h2[c, 0:blk, :] = (layer_norm(res) * (1.0 + mod_row(4, view)) + mod_row(3, view)).astype(BF16)
-        for dx, dy in DELTAS:
-            k = dx * HEADS_Y + dy
-            src, dst = h2.at[c, pl.ds(0, blk), :], h2.at[c, pl.ds(k * blk, blk), :]
-            g1_cps[c].append(rcopy(src, dst, ag1_s.at[k, c], ag1_r.at[k, c], head_dev(dx, dy)))
-            g1_cps[c][-1].start()
+        for dx, dy in SPREAD:
+            g1_cps[c].append(gather1(c, (0, 0), dx, dy))
+
+    def gather1(c, got, dx, dy):
+        held = got[0] * HEADS_Y + got[1]
+        k = (got[0] + dx) % HEADS_X * HEADS_Y + (got[1] + dy) % HEADS_Y
+        src, dst = h2.at[c, pl.ds(held * blk, blk), :], h2.at[c, pl.ds(k * blk, blk), :]
+        cp = rcopy(src, dst, ag1_s.at[k, c], ag1_r.at[k, c], head_dev(dx, dy))
+        cp.start()
+        return cp
+
+    def gather2(c, got, dx, dy):
+        k = (got[0] + dx) % HEADS_X * HEADS_Y + (got[1] + dy) % HEADS_Y
+        owner = head_peer(HEADS_X - got[0], HEADS_Y - got[1])
+        there = out_ref.at[rows_at(c * crows + owner * blk, blk), :]
+        src = fin.at[c] if got == (0, 0) else there
+        cp = rcopy(src, there, ag2_s.at[k, c], ag2_r.at[k, c], head_dev(dx, dy))
+        cp.start()
+        return cp
+
+    def forward(gather, cps, c):
+        for got, hops in FORWARDS:
+            cps[c][SPREAD.index(got)].wait_recv()
+            for dx, dy in hops:
+                cps[c].append(gather(c, got, dx, dy))
+
+    def arrived(cps, c):
+        for i, cp in enumerate(cps[c]):
+            if i >= len(SPREAD) or SPREAD[i] not in [got for got, _ in FORWARDS]:
+                cp.wait_recv()
 
     def feed_forward(c):
-        for cp in reversed(g1_cps[c]):
-            cp.wait_recv()
+        arrived(g1_cps, c)
         span = slice(c * crows, (c + 1) * crows)
         for n in range(ff // tile):
             at = slice(n * tile, (n + 1) * tile)
@@ -434,47 +489,36 @@
         for n in range(width // tile):
             at = slice(n * tile, (n + 1) * tile)
             part2[span, at] = dot_nn(hidden[span, :], downw[:, at]).astype(BF16)
-        for dx, dy in DELTAS:
-            bx, by = (HEADS_X - dx) % HEADS_X, (HEADS_Y - dy) % HEADS_Y
-            k = bx * HEADS_Y + by
-            src = part2.at[pl.ds(c * crows + k * blk, blk), :]
-            r2_cps[c].append(rcopy(src, rs2.at[k, c], rs2_s.at[k, c], rs2_r.at[k, c], head_dev(dx, dy)))
-            r2_cps[c][-1].start()
+        scatter_first(1, c)
 
     def finish(c):
         view = (c * crows + h * blk) // HD
-        total = part2[c * crows : c * crows + blk, :].astype(F32)
-        for cp in reversed(r2_cps[c]):
-            cp.wait_recv()
-        for k in range(1, n_head):
-            total = total + rs2[k, c].astype(F32)
+        total = scatter_sum(1, c)
         done = (resid[c] + mod_row(5, view) * total).astype(BF16)
         fin[c] = done
         mine = rows_at(c * crows + h * blk, blk)
         out_ref[mine, :] = done
-        for dx, dy in DELTAS:
-            k = dx * HEADS_Y + dy
-            g2_cps[c].append(rcopy(fin.at[c], out_ref.at[mine, :], ag2_s.at[k, c], ag2_r.at[k, c], head_dev(dx, dy)))
-            g2_cps[c][-1].start()
-
-    for c in ld_out:
+        for dx, dy in SPREAD:
+            g2_cps[c].append(gather2(c, (0, 0), dx, dy))
+
+    for c in ld_out + [ld_up, ld_down]:
         c.wait()
-    for c in range(CHUNKS):
-        for j in range(c * crows // HD, (c + 1) * crows // HD):
-            attention(j)
-        project(c)
-    for c in range(CHUNKS):
-        second_norm(c)
-    ld_up.wait()
-    ld_down.wait()
-    for c in range(CHUNKS):
-        feed_forward(c)
-    for c in range(CHUNKS):
-        finish(c)
-    for c in range(CHUNKS):
-        for cp in g2_cps[c]:
-            cp.wait_recv()
-    rest = [cp for phase in (r1_cps, g1_cps, r2_cps, g2_cps) for group in phase for cp in group]
+    stages = [
+        project,
+        functools.partial(scatter_second, 0),
+        second_norm,
+        functools.partial(forward, gather1, g1_cps),
+        feed_forward,
+        functools.partial(scatter_second, 1),
+        finish,
+        functools.partial(forward, gather2, g2_cps),
+        functools.partial(arrived, g2_cps),
+    ]
+    order = sorted((i + LAG * c, c, i) for i in range(len(stages)) for c in range(CHUNKS))
+    for _, c, i in order:
+        stages[i](c)
+    rest = [cp for phase in (g1_cps, g2_cps) for group in phase for cp in group]
+    rest += [cp for phase in rs_cps for group in phase for cp in group.values()]
     for c in mod_cps + kv_cps + fwd_cps + a_cps + b_cps + c_cps + rest:
         c.wait_send()
 
@@ -539,12 +583,12 @@
         vmem((HD, cols), BF16),
         vmem((rows, cols), BF16),
         vmem((rows, width), BF16),
-        vmem((n_head, CHUNKS, blk, width), BF16),
+        vmem((2, CHUNKS, 7, blk, width), BF16),
+        vmem((2, CHUNKS, 2, blk, width), BF16),
         vmem((CHUNKS, blk, width), F32),
         vmem((CHUNKS, n_head * blk, width), BF16),
         vmem((rows, ff), BF16),
         vmem((rows, width), BF16),
-        vmem((n_head, CHUNKS, blk, width), BF16),
         vmem((CHUNKS, blk, width), BF16),
         dma((21,)),
         dma((n_head,)),
@@ -557,15 +601,15 @@
         dma((n_z,)),
         dma((QUAD,)),
         dma((QUAD,)),
-    ] + [dma((n_head, CHUNKS))] * 8
+    ] + [dma((n_head, CHUNKS))] * 2 + [dma((2, CHUNKS, 7))] * 2 + [dma((n_head, CHUNKS))] * 2
     return pl.pallas_call(
         functools.partial(kernel, n_view),
         out_shape=jax.ShapeDtypeStruct((rows, width), BF16),
-        in_specs=[pl.BlockSpec(memory_space=pl.ANY)] * 11,
+        in_specs=[pl.BlockSpec(memory_space=pltpu.MemorySpace.HBM)] * 11,
         out_specs=pl.BlockSpec(memory_space=pltpu.VMEM),
         scratch_shapes=scratch,
         compiler_params=pltpu.CompilerParams(
-            collective_id=0, has_side_effects=True, vmem_limit_bytes=67043328
+            collective_id=0, has_side_effects=True, vmem_limit_bytes=64 * 1024 * 1024
         ),
         name="layer",
     )(

time: 71.6 us -> 69.8 us (0.975); the launches traced: 70.6 us -> 69.7 us
  Pallas kernels: 67.9 us -> 66.9 us
    pallas_call x1, Pallas kernels: 67.9 us -> 66.9 us  [body(): pl.pallas_call(functools.partial(kernel, n_view), out_shape=jax.ShapeDtyp...]
where the time goes in v4:
time: 69.8 us; the launch traced here: 69.7 us
  Pallas kernels  66.9 us (96%)
  local copies, waits for them, and re-layouts  2.06 us (3%)
    pallas_call x1, Pallas kernels, body(): pl.pallas_call(functools.partial(kernel, n_view), out_shape=jax.ShapeDtyp...  66.9 us
    unnamed x1, local copies, waits for them, and re-layouts  2.06 us

profile of v4, /device:TPU:2, one launch (start us, length us, event | category | flops | bytes accessed | tf_op | source)
XLA Modules:
  0.0 69.7 jit_solution(11151484348218112909)
XLA Ops:
  0.7 66.9 %layer.1 = bf16[256,1536]{1,0:T(8,128)(2,1)} custom-call(s32[4]{0:T(128)} %ts_hbm.1, f32[2,192]{1,0:T(2,128)} %gain_hbm.1, s32[4,6]{1,0:T(4,128)} %adj_hbm.1, s32[4]{0:T(128)} %cnt_hbm.1, s32[1]{0:T(128)S(6)} %copy.13.anc_hbm, bf16[256,1536]{1,0:T(8,128)(2,1)} %tok_hbm.1, bf16[1152,256]{1,0:T(8,128)(2,1)} %bitcast.5, bf16[3,192,1536]{2,1,0:T(8,128)(2,1)} %bitcast.4, ...), custom_call_target="tpu_custom_call" | custom-call | tf_op jit(solution)/shard_map/layer/pallas_call | solution.py:605
  67.6 2.1 %copy.14 = bf16[256,1536]{1,0:T(8,128)(2,1)} copy(bf16[256,1536]{1,0:T(8,128)(2,1)} %layer.1) | data formatting | bytes 1572864

commit v5 on v4

--- a/solution.py
+++ b/solution.py
@@ -22,10 +22,10 @@
 
 DELTAS = [(2, 1), (1, 1), (3, 1), (2, 0), (0, 1), (1, 0), (3, 0)]
 SPREAD = [(0, 1), (2, 0), (1, 0), (3, 0)]
-FORWARDS = [((0, 1), [(1, 0), (3, 0)]), ((2, 0), [(0, 1)])]
+FORWARDS = [((2, 0), [(0, 1)]), ((0, 1), [(1, 0), (3, 0)])]
 RELAYED = [(4, (2, 1), (0, 1)), (2, (1, 1), (1, 0)), (3, (3, 1), (3, 0))]
 DIRECT = [(0, (1, 0), (1, 0)), (1, (3, 0), (3, 0))]
-MIXED = [(6, (2, 0), (4,)), (5, (0, 1), (2, 3))]
+MIXED = [(5, (0, 1), (2, 3)), (6, (2, 0), (4,))]
 FINAL = [0, 1, 6, 5]
 LAG = 0.2
 
@@ -521,6 +521,10 @@
     rest += [cp for phase in rs_cps for group in phase for cp in group.values()]
     for c in mod_cps + kv_cps + fwd_cps + a_cps + b_cps + c_cps + rest:
         c.wait_send()
+
+
+def in_hbm(operand):
+    return pltpu.with_memory_space_constraint(operand, pltpu.MemorySpace.HBM)
 
 
 def body(
@@ -609,21 +613,16 @@
         out_specs=pl.BlockSpec(memory_space=pltpu.VMEM),
         scratch_shapes=scratch,
         compiler_params=pltpu.CompilerParams(
-            collective_id=0, has_side_effects=True, vmem_limit_bytes=64 * 1024 * 1024
+            collective_id=0, has_side_effects=True, vmem_limit_bytes=48 * 1024 * 1024
         ),
         name="layer",
     )(
-        timesteps,
-        qk_gain,
-        adjacency,
-        neighbour_count,
+        in_hbm(timesteps),
+        in_hbm(qk_gain),
+        in_hbm(adjacency),
+        in_hbm(neighbour_count),
         anchor,
-        tokens,
-        modw,
-        qkvw,
-        out_weight,
-        up_weight,
-        down_weight,
+        *(in_hbm(operand) for operand in (tokens, modw, qkvw, out_weight, up_weight, down_weight)),
     )
 
 

time: 69.8 us -> 67.9 us (0.973)
  local copies, waits for them, and re-layouts: 2.06 us -> 0.88 us
    unnamed x1, local copies, waits for them, and re-layouts: 2.06 us -> 0.88 us
where the time goes in v5:
time: 67.9 us; the launch traced here: 67.8 us
  Pallas kernels  66.3 us (98%)
  local copies, waits for them, and re-layouts  0.88 us (1%)
    pallas_call x1, Pallas kernels, body(): pl.pallas_call(functools.partial(kernel, n_view), out_shape=jax.ShapeDtyp...  66.3 us

profile of v5, /device:TPU:2, one launch (start us, length us, event | category | flops | bytes accessed | tf_op | source)
XLA Modules:
  0.0 67.8 jit_solution(16242929430522934562)
XLA Ops:
  0.7 66.3 %layer.1 = bf16[256,1536]{1,0:T(8,128)(2,1)S(1)} custom-call(s32[4]{0:T(128)} %ts_hbm.1, f32[2,192]{1,0:T(2,128)} %gain_hbm.1, s32[4,6]{1,0:T(4,128)} %adj_hbm.1, s32[4]{0:T(128)} %cnt_hbm.1, s32[1]{0:T(128)S(6)} %copy.13.anc_hbm, bf16[256,1536]{1,0:T(8,128)(2,1)} %tok_hbm.1, bf16[1152,256]{1,0:T(8,128)(2,1)} %bitcast.5, bf16[3,192,1536]{2,1,0:T(8,128)(2,1)} %bitcast.4, ...), custom_call_target="tpu_custom_call" | custom-call | tf_op jit(solution)/shard_map/layer/pallas_call | solution.py:609
  66.9 0.9 %copy.14 = bf16[256,1536]{1,0:T(8,128)(2,1)} copy(bf16[256,1536]{1,0:T(8,128)(2,1)S(1)} %layer.1) | data formatting | bytes 1572864
